TPU v7x, 256 devices: a whole 4x4x8 slice. The times are simulated.
256 devices in a mesh: seq: 64 (over z, y, core), chan: 4 (over x).
Axes of the slice: x: 4, y: 4, z: 8, core: 2. Of those that a mesh axis runs over, the one named last changes fastest.
Arguments:
- features: bfloat16 [32768, 512], P('seq', 'chan'), may hold values from -600 to 600
- pre_gate: bfloat16 [32768, 512], P('seq', 'chan'), may hold values from -6 to 6
- post_gate: bfloat16 [32768, 512], P('seq', 'chan'), may hold values from -6 to 6
- norm_gain: float32 [512], P('chan'), may hold values from 0.1 to 1.9
- skip_weight: float32 [512], P('chan'), may hold values from -4 to 4
- spectrum: float32 [2, 128, 512, 512], P(None, 'seq', None, 'chan'), may hold values from -6 to 6
Outputs:
- gated_out: bfloat16 [32768, 512], P('seq', 'chan')
All inputs are finite; a program needn't handle non-finite values.
Results may differ from a plain program's by a relative error of at most 0.007.
Values may be sent and summed in bfloat16 or wider, within the bound.
A program may use at most 64 MiB of HBM per device.

v0:
```python
import math
import jax
import jax.numpy as jnp
import numpy as np
from jax import lax
from jax.sharding import PartitionSpec as P

CHANNELS = 512
ROW_GROUP = 4
PRECISE = lax.Precision.HIGHEST
FULL_TURN = 2.0 * math.pi


def reversed_digits(count):
    levels = count.bit_length() - 1
    positions = np.arange(count)
    result = np.zeros(count, np.int64)
    for bit_pos in range(levels):
        result = result + ((positions >> bit_pos & 1) << levels - 1 - bit_pos)
    return result


def rotation(numerator, denominator):
    angle = (numerator % denominator).astype(jnp.float32) * (FULL_TURN / denominator)
    return (jnp.cos(angle), jnp.sin(angle))


def mm(spec, left, right):
    return jnp.einsum(spec, left, right, precision=PRECISE, preferred_element_type=jnp.float32)


def local(features, pre_gate, post_gate, norm_gain, skip_weight, spectrum):
    tok_rows, chan_width = features.shape
    seq_count = lax.axis_size("seq")
    stride = 2 * seq_count
    all_bins = stride * tok_rows
    group = chan_width // seq_count
    first_len = stride * ROW_GROUP
    second_len = all_bins // first_len
    half_first = first_len // 2
    spec_rows = spectrum.reshape(2, 2, second_len, ROW_GROUP, chan_width)
    spec_rows = jnp.transpose(spec_rows, (4, 0, 1, 3, 2))
    spec_chan = lax.all_to_all(spec_rows, "seq", 0, 2, tiled=True)
    spec_chan = spec_chan.reshape(group, 2, first_len, second_len)
    widened = features.astype(jnp.float32)
    squares = lax.psum(jnp.sum(widened * widened, axis=1), "chan")
    scaled = widened * lax.rsqrt(squares / CHANNELS + 1e-06)[:, None] * norm_gain
    signal = (scaled * pre_gate.astype(jnp.float32)).astype(jnp.bfloat16)
    sig_chan = lax.all_to_all(signal.T, "seq", 0, 1, tiled=True)
    sig_chan = sig_chan.astype(jnp.float32).reshape(group, half_first, second_len)
    digit_order = reversed_digits(seq_count)
    slots = np.arange(stride)
    low_bins = 2 * digit_order[slots // 2] + slots % 2
    row_bins = (low_bins[:, None] + stride * np.arange(ROW_GROUP)[None, :]).reshape(-1)
    row_bins = jnp.asarray(row_bins.astype(np.int32))
    first_in = jnp.arange(half_first, dtype=jnp.int32)
    cos_first, sin_first = rotation(row_bins[:, None] * first_in[None, :], first_len)
    second_in = jnp.arange(second_len, dtype=jnp.int32)
    cos_twist, sin_twist = rotation(row_bins[:, None] * second_in[None, :], all_bins)
    cos_second, sin_second = rotation(second_in[:, None] * second_in[None, :], second_len)
    part_re = mm("rn,cnm->crm", cos_first, sig_chan)
    part_im = -mm("rn,cnm->crm", sin_first, sig_chan)
    twist_re = part_re * cos_twist + part_im * sin_twist
    twist_im = part_im * cos_twist - part_re * sin_twist
    freq_re = mm("crn,nk->crk", twist_re, cos_second) + mm("crn,nk->crk", twist_im, sin_second)
    freq_im = mm("crn,nk->crk", twist_im, cos_second) - mm("crn,nk->crk", twist_re, sin_second)
    filt_re = spec_chan[:, 0]
    filt_im = spec_chan[:, 1]
    prod_re = freq_re * filt_re - freq_im * filt_im
    prod_im = freq_re * filt_im + freq_im * filt_re
    back_re = mm("crk,kn->crn", prod_re, cos_second) - mm("crk,kn->crn", prod_im, sin_second)
    back_im = mm("crk,kn->crn", prod_im, cos_second) + mm("crk,kn->crn", prod_re, sin_second)
    untwist_re = back_re * cos_twist - back_im * sin_twist
    untwist_im = back_im * cos_twist + back_re * sin_twist
    conv = mm("rn,crm->cnm", cos_first, untwist_re) - mm("rn,crm->cnm", sin_first, untwist_im)
    conv = (conv * (1.0 / all_bins)).reshape(group, seq_count * tok_rows)
    result = lax.all_to_all(conv, "seq", 1, 0, tiled=True).T
    gated = post_gate.astype(jnp.float32) * (result + skip_weight * signal.astype(jnp.float32))
    return gated.astype(jnp.bfloat16)


def solution(mesh):
    return jax.shard_map(
        local,
        mesh=mesh,
        in_specs=(
            P("seq", "chan"),
            P("seq", "chan"),
            P("seq", "chan"),
            P("chan"),
            P("chan"),
            P(None, "seq", None, "chan"),
        ),
        out_specs=P("seq", "chan"),
        check_vma=False,
    )
```

profile of v0, /device:TPU:1, one launch (start us, length us, event | category | flops | bytes accessed | tf_op | source)
XLA Modules:
  0.0 104.2 jit_solution(3268081029509111856)
XLA Ops:
  0.0 0.0 copy-start.2
  0.0 0.0 copy-start.1
  0.0 1.1 %copy.75 = bf16[512,128]{0,1:T(8,128)(2,1)S(1)} copy(bf16[512,128]{1,0:T(8,128)(2,1)} %param.8) | data formatting | bytes 262144 | tf_op args[1]
  1.1 0.0 copy-done.2
  1.1 0.1 copy.74
  1.3 9.3 %psum.7 = f32[512]{0:T(512)S(1)} all-reduce(f32[512]{0:T(512)S(1)} %fusion.20), channel_id=1, replica_groups=mesh['seq'=64,'chan'=4] {'chan'}, use_global_device_ids=true, to_apply=%region_1.0 | all-reduce | flops 512 | bytes 4096 | tf_op jit(solution)/shard_map/psum | solution.py:46
  10.6 0.8 fusion.120
  11.4 0.7 all_to_all.37
  12.1 14.3 %all-to-all-start = ((bf16[64,2,512]{2,1,0:T(2,128)(2,1)}), bf16[64,2,512]{2,1,0:T(2,128)(2,1)S(1)}, u32[]{:S(2)}, u32[]{:S(2)}) async-start(bf16[64,2,512]{2,1,0:T(2,128)(2,1)} %all_to_all.37), calls=%async_computation | async-start | bytes 262144 | tf_op jit(solution)/shard_map/all_to_all | solution.py:49
  26.4 0.0 copy-done.1
  26.4 1.3 %copy.81 = f32[128,2,2,4,128]{4,3,2,1,0:T(4,128)} copy(f32[128,2,2,4,128]{0,3,4,2,1:T(4,128)S(1)} %bitcast.73) | data formatting | bytes 2097152 | tf_op jit(solution)/shard_map/transpose | solution.py:42
  27.8 0.0 copy-start.4
  27.8 9.8 %all-to-all-done = bf16[64,2,512]{2,1,0:T(2,128)(2,1)S(1)} async-done(((bf16[64,2,512]{2,1,0:T(2,128)(2,1)}), bf16[64,2,512]{2,1,0:T(2,128)(2,1)S(1)}, u32[]{:S(2)}, u32[]{:S(2)}) %all-to-all-start) | async-done | bytes 131104 | tf_op jit(solution)/shard_map/all_to_all | solution.py:49
  37.5 4.5 %all-to-all-start.1 = ((f32[128,2,2,4,128]{4,3,2,1,0:T(4,128)}), f32[128,2,2,4,128]{4,3,2,1,0:T(4,128)S(1)}, u32[]{:S(2)}, u32[]{:S(2)}) async-start(f32[128,2,2,4,128]{4,3,2,1,0:T(4,128)} %copy.81), calls=%async_computation.1 | async-start | bytes 2097152 | tf_op jit(solution)/shard_map/all_to_all | solution.py:43
  42.0 0.0 copy-done.4
  42.0 1.0 fusion.43
  43.1 0.1 reshape.68
  43.2 3.1 %fusion = f32[2,512,128]{1,2,0:T(8,128)S(1)} fusion(bf16[2,256,128]{2,1,0:T(8,128)(2,1)S(1)} %reshape.68, s32[512]{0:T(512)S(1)} %copy-done.4), kind=kOutput, calls=%fused_computation.1 | convolution fusion | flops 404619264 | bytes 657408 | tf_op jit(solution)/shard_map/rn,cnm->crm/dot_general | solution.py:29
  46.3 3.2 %convolution_bitcast_fusion = f32[2,512,128]{1,2,0:T(8,128)S(1)} fusion(bf16[2,256,128]{2,1,0:T(8,128)(2,1)S(1)} %reshape.68, s32[512]{0:T(512)S(1)} %copy-done.4), kind=kOutput, calls=%fused_computation.2 | convolution fusion | flops 404488192 | bytes 657408 | tf_op jit(solution)/shard_map/rn,cnm->crm/dot_general | solution.py:29
  49.5 1.2 %fusion.57 = f32[2,512,128]{2,1,0:T(8,128)S(1)} fusion(f32[2,512,128]{1,2,0:T(8,128)S(1)} %fusion, f32[2,512,128]{1,2,0:T(8,128)S(1)} %convolution_bitcast_fusion, f32[512,128]{0,1:T(8,128)S(1)} %get-tuple-element.8, f32[512,128]{0,1:T(8,128)S(1)} %get-tuple-element.7), kind=kOutput, calls=%fused_computation.78 | convolution fusion | flops 201949184 | bytes 2097152 | tf_op jit(solution)/shard_map/crn,nk->crk/dot_general | solution.py:29
  50.8 2.1 %fusion.55 = f32[2,512,128]{2,1,0:T(8,128)} fusion(f32[2,512,128]{1,2,0:T(8,128)S(1)} %convolution_bitcast_fusion, f32[2,512,128]{1,2,0:T(8,128)S(1)} %fusion, f32[512,128]{0,1:T(8,128)S(1)} %get-tuple-element.8, f32[512,128]{0,1:T(8,128)S(1)} %get-tuple-element.7), kind=kOutput, calls=%fused_computation.76 | convolution fusion | flops 201949184 | bytes 2097152 | tf_op jit(solution)/shard_map/crn,nk->crk/dot_general | solution.py:29
  52.8 1.2 %convolution_add_fusion.1 = f32[2,512,128]{2,1,0:T(8,128)S(1)} fusion(f32[2,512,128]{2,1,0:T(8,128)S(1)} %fusion.57, f32[2,512,128]{1,2,0:T(8,128)S(1)} %convolution_bitcast_fusion, f32[2,512,128]{1,2,0:T(8,128)S(1)} %fusion, f32[512,128]{0,1:T(8,128)S(1)} %get-tuple-element.8, f32[512,128]{0,1:T(8,128)S(1)} %get-tuple-element.7), kind=kOutput, calls=%fused_computation.6 | convolution fusion | flops 202080256 | bytes 2621440 | tf_op jit(solution)/shard_map/crn,nk->crk/dot_general | solution.py:29
  54.1 16.1 %all-to-all-done.1 = f32[128,2,2,4,128]{4,3,2,1,0:T(4,128)S(1)} async-done(((f32[128,2,2,4,128]{4,3,2,1,0:T(4,128)}), f32[128,2,2,4,128]{4,3,2,1,0:T(4,128)S(1)}, u32[]{:S(2)}, u32[]{:S(2)}) %all-to-all-start.1) | async-done | bytes 1048608 | tf_op jit(solution)/shard_map/all_to_all | solution.py:43
  70.2 0.3 copy.82
  70.5 0.0 copy-start
  70.5 0.7 copy.83
  71.2 0.3 copy-done
  71.6 1.2 %multiply_subtract_fusion = (f32[2,512,128]{2,1,0:T(8,128)S(1)}, f32[2,512,128]{2,1,0:T(8,128)S(1)}) fusion(f32[2,512,128]{2,1,0:T(8,128)S(1)} %convolution_add_fusion.1, f32[2,2,512,128]{3,2,0,1:T(8,128)S(1)} %bitcast.72, f32[2,512,128]{2,1,0:T(8,128)S(1)} %copy-done, f32[2,512,128]{1,2,0:T(8,128)S(1)} %fusion, ...), kind=kOutput, calls=%fused_computation.30 | convolution fusion | flops 202866688 | bytes 4718592 | tf_op jit(solution)/shard_map/crn,nk->crk/dot_general | solution.py:29
  72.8 0.9 fusion.51
  73.7 0.9 fusion.53
  74.6 0.9 convolution_add_fusion
  75.4 0.9 convolution_subtract_fusion
  76.3 2.8 %fusion.8 = f32[2,128,256]{2,1,0:T(8,128)S(1)} fusion(f32[2,512,128]{1,2,0:T(8,128)S(1)} %convolution_add_fusion, f32[2,512,128]{1,2,0:T(8,128)S(1)} %convolution_subtract_fusion, f32[512,128]{0,1:T(8,128)S(1)} %get-tuple-element.8, f32[512,128]{0,1:T(8,128)S(1)} %get-tuple-element.7, s32[512]{0:T(512)S(1)} %copy-done.4), kind=kOutput, calls=%fused_computation.20 | convolution fusion | flops 404881408 | bytes 1837056 | tf_op jit(solution)/shard_map/rn,crm->cnm/dot_general | solution.py:29
  79.2 2.6 %fusion.2 = f32[2,256,128]{1,2,0:T(8,128)S(1)} fusion(f32[2,128,256]{2,1,0:T(8,128)S(1)} %fusion.8, f32[2,512,128]{1,2,0:T(8,128)S(1)} %convolution_subtract_fusion, f32[2,512,128]{1,2,0:T(8,128)S(1)} %convolution_add_fusion, f32[512,128]{0,1:T(8,128)S(1)} %get-tuple-element.8, f32[512,128]{0,1:T(8,128)S(1)} %get-tuple-element.7, s32[512]{0:T(512)S(1)} %copy-done.4), kind=kOutput, calls=%fused_computation.9 | convolution fusion | flops 405012480 | bytes 2099200 | tf_op jit(solution)/shard_map/rn,crm->cnm/dot_general | solution.py:29
  81.8 0.1 copy.90
  81.9 0.9 copy.91
  82.9 0.0 copy-start.3
  82.9 6.5 %all-to-all-start.2 = ((f32[2,64,512]{2,0,1:T(2,128)}), f32[2,64,512]{2,0,1:T(2,128)S(1)}, u32[]{:S(2)}, u32[]{:S(2)}) async-start(f32[2,64,512]{2,0,1:T(2,128)} %copy.91), calls=%async_computation.2 | async-start | bytes 524288 | tf_op jit(solution)/shard_map/all_to_all | solution.py:77
  89.4 0.0 copy-done.3
  89.4 0.1 copy.73
  89.5 13.0 %all-to-all-done.2 = f32[2,64,512]{2,0,1:T(2,128)S(1)} async-done(((f32[2,64,512]{2,0,1:T(2,128)}), f32[2,64,512]{2,0,1:T(2,128)S(1)}, u32[]{:S(2)}, u32[]{:S(2)}) %all-to-all-start.2) | async-done | bytes 262176 | tf_op jit(solution)/shard_map/all_to_all | solution.py:77
  102.6 0.0 copy-start.5
  102.6 0.0 copy-start.6
  102.6 0.2 all_to_all.46
  102.8 0.5 copy-done.5
  103.2 0.0 copy-done.6
  103.2 0.1 fusion.28
  103.4 0.8 copy.92
  (4 shorter events, 0.1 us)
Async XLA Ops:
  0.0 1.1 %copy-start.2 = (bf16[512,128]{1,0:T(8,128)(2,1)S(1)}, bf16[512,128]{1,0:T(8,128)(2,1)}, u32[]{:S(2)}) copy-start(bf16[512,128]{1,0:T(8,128)(2,1)} %param.7) | copy-start | bytes 393220
  0.0 26.4 %copy-start.1 = (f32[2,2,512,128]{3,2,1,0:T(8,128)S(1)}, f32[2,2,512,128]{3,2,1,0:T(8,128)}, u32[]{:S(2)}) copy-start(f32[2,2,512,128]{3,2,1,0:T(8,128)} %param.12) | copy-start | bytes 3145732
  12.1 25.5 %all-to-all-start = ((bf16[64,2,512]{2,1,0:T(2,128)(2,1)}), bf16[64,2,512]{2,1,0:T(2,128)(2,1)S(1)}, u32[]{:S(2)}, u32[]{:S(2)}) async-start(bf16[64,2,512]{2,1,0:T(2,128)(2,1)} %all_to_all.37), calls=%async_computation | async-start | bytes 262144 | tf_op jit(solution)/shard_map/all_to_all | solution.py:49
  27.8 14.3 %copy-start.4 = (s32[512]{0:T(512)S(1)}, s32[512]{0:T(512)}, u32[]{:S(2)}) copy-start(s32[512]{0:T(512)} %constant.60.clone) | copy-start | bytes 6148
  37.5 32.6 %all-to-all-start.1 = ((f32[128,2,2,4,128]{4,3,2,1,0:T(4,128)}), f32[128,2,2,4,128]{4,3,2,1,0:T(4,128)S(1)}, u32[]{:S(2)}, u32[]{:S(2)}) async-start(f32[128,2,2,4,128]{4,3,2,1,0:T(4,128)} %copy.81), calls=%async_computation.1 | async-start | bytes 2097152 | tf_op jit(solution)/shard_map/all_to_all | solution.py:43
  70.5 1.0 %copy-start = (f32[2,512,128]{2,1,0:T(8,128)S(1)}, f32[2,512,128]{2,1,0:T(8,128)}, u32[]{:S(2)}) copy-start(f32[2,512,128]{2,1,0:T(8,128)} %fusion.55) | copy-start | bytes 1572868
  82.9 6.6 %copy-start.3 = (bf16[512,128]{1,0:T(8,128)(2,1)S(1)}, bf16[512,128]{1,0:T(8,128)(2,1)}, u32[]{:S(2)}) copy-start(bf16[512,128]{1,0:T(8,128)(2,1)} %param.9) | copy-start | bytes 393220
  82.9 19.7 %all-to-all-start.2 = ((f32[2,64,512]{2,0,1:T(2,128)}), f32[2,64,512]{2,0,1:T(2,128)S(1)}, u32[]{:S(2)}, u32[]{:S(2)}) async-start(f32[2,64,512]{2,0,1:T(2,128)} %copy.91), calls=%async_computation.2 | async-start | bytes 524288 | tf_op jit(solution)/shard_map/all_to_all | solution.py:77
  102.6 0.7 copy-start.5
  102.6 0.7 copy-start.6
where the time goes:
time: 105 us; the launch traced here: 104 us
  waiting for transfers between devices  38.9 us (37%)
  starting transfers between devices  25.4 us (24%)
  matrix products  21 us (20%)
  blocking collectives  9.3 us (9%)
  local copies, waits for them, and re-layouts  7.36 us (7%)
  other arithmetic  1.99 us (2%)
    dot_general x12, matrix products, mm(): jnp.einsum(spec, left, right, precision=PRECISE, preferred_element_type=j...  21 us
    all_to_all x1, waiting for transfers between devices, local(): spec_chan = lax.all_to_all(spec_rows, 'seq', 0, 2, tiled=True)  16.1 us
    all_to_all x1, starting transfers between devices, local(): sig_chan = lax.all_to_all(signal.T, 'seq', 0, 1, tiled=True)  14.3 us
    all_to_all x1, waiting for transfers between devices, local(): result = lax.all_to_all(conv, 'seq', 1, 0, tiled=True).T  13 us
    all_to_all x1, waiting for transfers between devices, local(): sig_chan = lax.all_to_all(signal.T, 'seq', 0, 1, tiled=True)  9.77 us
    psum x1, blocking collectives, local(): squares = lax.psum(jnp.sum(widened * widened, axis=1), 'chan')  9.3 us
    all_to_all x1, starting transfers between devices, local(): result = lax.all_to_all(conv, 'seq', 1, 0, tiled=True).T  6.55 us
    all_to_all x1, starting transfers between devices, local(): spec_chan = lax.all_to_all(spec_rows, 'seq', 0, 2, tiled=True)  4.48 us
  transfers between devices with their start and end apart: 3, of which 3 were waited for; matrix products, arithmetic and copies ran while one was open for 13% of the time, Pallas kernels for 0%

commit v1 on v0

--- a/solution.py
+++ b/solution.py
@@ -43,7 +43,7 @@
     spec_chan = lax.all_to_all(spec_rows, "seq", 0, 2, tiled=True)
     spec_chan = spec_chan.reshape(group, 2, first_len, second_len)
     widened = features.astype(jnp.float32)
-    squares = lax.psum(jnp.sum(widened * widened, axis=1), "chan")
+    squares = jnp.sum(lax.all_gather(jnp.sum(widened * widened, axis=1), "chan"), axis=0)
     scaled = widened * lax.rsqrt(squares / CHANNELS + 1e-06)[:, None] * norm_gain
     signal = (scaled * pre_gate.astype(jnp.float32)).astype(jnp.bfloat16)
     sig_chan = lax.all_to_all(signal.T, "seq", 0, 1, tiled=True)

time: 105 us -> 105 us (level)
    psum x1 -> x0, blocking collectives: 9.3 us -> none  [local(): squares = lax.psum(jnp.sum(widened * widened, axis=1), 'chan')]
    all_gather x0 -> x1, blocking collectives: none -> 9.26 us  [local(): lax.all_gather(jnp.sum(widened * widened, axis=1), 'chan')]
where the time goes in v1:
time: 105 us
  waiting for transfers between devices  38.9 us (37%)
  starting transfers between devices  26 us (25%)
  matrix products  21 us (20%)
  blocking collectives  9.26 us (9%)
  local copies, waits for them, and re-layouts  7.36 us (7%)
  other arithmetic  2.01 us (2%)
    dot_general x12, matrix products, mm(): jnp.einsum(spec, left, right, precision=PRECISE, preferred_element_type=j...  21 us
    all_to_all x1, waiting for transfers between devices, local(): spec_chan = lax.all_to_all(spec_rows, 'seq', 0, 2, tiled=True)  16.1 us
    all_to_all x1, starting transfers between devices, local(): sig_chan = lax.all_to_all(signal.T, 'seq', 0, 1, tiled=True)  15 us
    all_to_all x1, waiting for transfers between devices, local(): result = lax.all_to_all(conv, 'seq', 1, 0, tiled=True).T  13 us
    all_to_all x1, waiting for transfers between devices, local(): sig_chan = lax.all_to_all(signal.T, 'seq', 0, 1, tiled=True)  9.77 us
    all_gather x1, blocking collectives, local(): lax.all_gather(jnp.sum(widened * widened, axis=1), 'chan')  9.26 us
    all_to_all x1, starting transfers between devices, local(): result = lax.all_to_all(conv, 'seq', 1, 0, tiled=True).T  6.54 us
    all_to_all x1, starting transfers between devices, local(): spec_chan = lax.all_to_all(spec_rows, 'seq', 0, 2, tiled=True)  4.48 us
  transfers between devices with their start and end apart: 3, of which 3 were waited for; matrix products, arithmetic and copies ran while one was open for 13% of the time, Pallas kernels for 0%

profile of v1, /device:TPU:1, one launch (start us, length us, event | category | flops | bytes accessed | tf_op | source)
XLA Modules:
  0.0 104.8 jit_solution(1699162480549974867)
XLA Ops:
  0.0 0.0 copy-start.2
  0.0 0.0 copy-start.1
  0.0 1.1 %copy.75 = bf16[512,128]{0,1:T(8,128)(2,1)S(1)} copy(bf16[512,128]{1,0:T(8,128)(2,1)} %param.8) | data formatting | bytes 262144 | tf_op args[1]
  1.1 0.0 copy-done.2
  1.1 0.1 copy.74
  1.3 9.3 %all-gather.1 = f32[4,1,512]{2,1,0:T(1,128)S(1)} all-gather(f32[1,1,512]{2,1,0:T(1,128)S(1)} %bitcast.77), channel_id=2, replica_groups=mesh['seq'=64,'chan'=4] {'chan'}, dimensions={0}, use_global_device_ids=true | all-gather | bytes 10240 | tf_op jit(solution)/shard_map/all_gather | solution.py:46
  10.6 0.8 fusion.120
  11.3 0.7 all_to_all.37
  12.1 15.0 %all-to-all-start = ((bf16[64,2,512]{2,1,0:T(2,128)(2,1)}), bf16[64,2,512]{2,1,0:T(2,128)(2,1)S(1)}, u32[]{:S(2)}, u32[]{:S(2)}) async-start(bf16[64,2,512]{2,1,0:T(2,128)(2,1)} %all_to_all.37), calls=%async_computation | async-start | bytes 262144 | tf_op jit(solution)/shard_map/all_to_all | solution.py:49
  27.0 0.0 copy-done.1
  27.1 1.3 %copy.81 = f32[128,2,2,4,128]{4,3,2,1,0:T(4,128)} copy(f32[128,2,2,4,128]{0,3,4,2,1:T(4,128)S(1)} %bitcast.74) | data formatting | bytes 2097152 | tf_op jit(solution)/shard_map/transpose | solution.py:42
  28.4 0.0 copy-start.4
  28.4 9.8 %all-to-all-done = bf16[64,2,512]{2,1,0:T(2,128)(2,1)S(1)} async-done(((bf16[64,2,512]{2,1,0:T(2,128)(2,1)}), bf16[64,2,512]{2,1,0:T(2,128)(2,1)S(1)}, u32[]{:S(2)}, u32[]{:S(2)}) %all-to-all-start) | async-done | bytes 131104 | tf_op jit(solution)/shard_map/all_to_all | solution.py:49
  38.2 4.5 %all-to-all-start.1 = ((f32[128,2,2,4,128]{4,3,2,1,0:T(4,128)}), f32[128,2,2,4,128]{4,3,2,1,0:T(4,128)S(1)}, u32[]{:S(2)}, u32[]{:S(2)}) async-start(f32[128,2,2,4,128]{4,3,2,1,0:T(4,128)} %copy.81), calls=%async_computation.1 | async-start | bytes 2097152 | tf_op jit(solution)/shard_map/all_to_all | solution.py:43
  42.6 0.0 copy-done.4
  42.7 1.0 fusion.43
  43.7 0.1 reshape.72
  43.8 3.1 %fusion = f32[2,512,128]{1,2,0:T(8,128)S(1)} fusion(bf16[2,256,128]{2,1,0:T(8,128)(2,1)S(1)} %reshape.72, s32[512]{0:T(512)S(1)} %copy-done.4), kind=kOutput, calls=%fused_computation.1 | convolution fusion | flops 404619264 | bytes 657408 | tf_op jit(solution)/shard_map/rn,cnm->crm/dot_general | solution.py:29
  46.9 3.2 %convolution_bitcast_fusion = f32[2,512,128]{1,2,0:T(8,128)S(1)} fusion(bf16[2,256,128]{2,1,0:T(8,128)(2,1)S(1)} %reshape.72, s32[512]{0:T(512)S(1)} %copy-done.4), kind=kOutput, calls=%fused_computation.2 | convolution fusion | flops 404488192 | bytes 657408 | tf_op jit(solution)/shard_map/rn,cnm->crm/dot_general | solution.py:29
  50.1 1.2 %fusion.57 = f32[2,512,128]{2,1,0:T(8,128)S(1)} fusion(f32[2,512,128]{1,2,0:T(8,128)S(1)} %fusion, f32[2,512,128]{1,2,0:T(8,128)S(1)} %convolution_bitcast_fusion, f32[512,128]{0,1:T(8,128)S(1)} %get-tuple-element.8, f32[512,128]{0,1:T(8,128)S(1)} %get-tuple-element.7), kind=kOutput, calls=%fused_computation.78 | convolution fusion | flops 201949184 | bytes 2097152 | tf_op jit(solution)/shard_map/crn,nk->crk/dot_general | solution.py:29
  51.4 2.1 %fusion.55 = f32[2,512,128]{2,1,0:T(8,128)} fusion(f32[2,512,128]{1,2,0:T(8,128)S(1)} %convolution_bitcast_fusion, f32[2,512,128]{1,2,0:T(8,128)S(1)} %fusion, f32[512,128]{0,1:T(8,128)S(1)} %get-tuple-element.8, f32[512,128]{0,1:T(8,128)S(1)} %get-tuple-element.7), kind=kOutput, calls=%fused_computation.76 | convolution fusion | flops 201949184 | bytes 2097152 | tf_op jit(solution)/shard_map/crn,nk->crk/dot_general | solution.py:29
  53.5 1.2 %convolution_add_fusion.1 = f32[2,512,128]{2,1,0:T(8,128)S(1)} fusion(f32[2,512,128]{2,1,0:T(8,128)S(1)} %fusion.57, f32[2,512,128]{1,2,0:T(8,128)S(1)} %convolution_bitcast_fusion, f32[2,512,128]{1,2,0:T(8,128)S(1)} %fusion, f32[512,128]{0,1:T(8,128)S(1)} %get-tuple-element.8, f32[512,128]{0,1:T(8,128)S(1)} %get-tuple-element.7), kind=kOutput, calls=%fused_computation.6 | convolution fusion | flops 202080256 | bytes 2621440 | tf_op jit(solution)/shard_map/crn,nk->crk/dot_general | solution.py:29
  54.7 16.1 %all-to-all-done.1 = f32[128,2,2,4,128]{4,3,2,1,0:T(4,128)S(1)} async-done(((f32[128,2,2,4,128]{4,3,2,1,0:T(4,128)}), f32[128,2,2,4,128]{4,3,2,1,0:T(4,128)S(1)}, u32[]{:S(2)}, u32[]{:S(2)}) %all-to-all-start.1) | async-done | bytes 1048608 | tf_op jit(solution)/shard_map/all_to_all | solution.py:43
  70.8 0.3 copy.82
  71.1 0.0 copy-start
  71.1 0.7 copy.83
  71.8 0.3 copy-done
  72.2 1.2 %multiply_subtract_fusion = (f32[2,512,128]{2,1,0:T(8,128)S(1)}, f32[2,512,128]{2,1,0:T(8,128)S(1)}) fusion(f32[2,512,128]{2,1,0:T(8,128)S(1)} %convolution_add_fusion.1, f32[2,2,512,128]{3,2,0,1:T(8,128)S(1)} %bitcast.73, f32[2,512,128]{2,1,0:T(8,128)S(1)} %copy-done, f32[2,512,128]{1,2,0:T(8,128)S(1)} %fusion, ...), kind=kOutput, calls=%fused_computation.30 | convolution fusion | flops 202866688 | bytes 4718592 | tf_op jit(solution)/shard_map/crn,nk->crk/dot_general | solution.py:29
  73.4 0.9 fusion.51
  74.3 0.9 fusion.53
  75.2 0.9 convolution_add_fusion
  76.1 0.9 convolution_subtract_fusion
  76.9 2.8 %fusion.8 = f32[2,128,256]{2,1,0:T(8,128)S(1)} fusion(f32[2,512,128]{1,2,0:T(8,128)S(1)} %convolution_add_fusion, f32[2,512,128]{1,2,0:T(8,128)S(1)} %convolution_subtract_fusion, f32[512,128]{0,1:T(8,128)S(1)} %get-tuple-element.8, f32[512,128]{0,1:T(8,128)S(1)} %get-tuple-element.7, s32[512]{0:T(512)S(1)} %copy-done.4), kind=kOutput, calls=%fused_computation.20 | convolution fusion | flops 404881408 | bytes 1837056 | tf_op jit(solution)/shard_map/rn,crm->cnm/dot_general | solution.py:29
  79.8 2.6 %fusion.2 = f32[2,256,128]{1,2,0:T(8,128)S(1)} fusion(f32[2,128,256]{2,1,0:T(8,128)S(1)} %fusion.8, f32[2,512,128]{1,2,0:T(8,128)S(1)} %convolution_subtract_fusion, f32[2,512,128]{1,2,0:T(8,128)S(1)} %convolution_add_fusion, f32[512,128]{0,1:T(8,128)S(1)} %get-tuple-element.8, f32[512,128]{0,1:T(8,128)S(1)} %get-tuple-element.7, s32[512]{0:T(512)S(1)} %copy-done.4), kind=kOutput, calls=%fused_computation.9 | convolution fusion | flops 405012480 | bytes 2099200 | tf_op jit(solution)/shard_map/rn,crm->cnm/dot_general | solution.py:29
  82.4 0.1 copy.90
  82.6 0.9 copy.91
  83.5 0.0 copy-start.3
  83.5 6.5 %all-to-all-start.2 = ((f32[2,64,512]{2,0,1:T(2,128)}), f32[2,64,512]{2,0,1:T(2,128)S(1)}, u32[]{:S(2)}, u32[]{:S(2)}) async-start(f32[2,64,512]{2,0,1:T(2,128)} %copy.91), calls=%async_computation.2 | async-start | bytes 524288 | tf_op jit(solution)/shard_map/all_to_all | solution.py:77
  90.0 0.0 copy-done.3
  90.0 0.1 copy.73
  90.1 13.0 %all-to-all-done.2 = f32[2,64,512]{2,0,1:T(2,128)S(1)} async-done(((f32[2,64,512]{2,0,1:T(2,128)}), f32[2,64,512]{2,0,1:T(2,128)S(1)}, u32[]{:S(2)}, u32[]{:S(2)}) %all-to-all-start.2) | async-done | bytes 262176 | tf_op jit(solution)/shard_map/all_to_all | solution.py:77
  103.2 0.0 copy-start.5
  103.2 0.0 copy-start.6
  103.2 0.2 all_to_all.46
  103.4 0.5 copy-done.5
  103.8 0.0 copy-done.6
  103.8 0.1 fusion.28
  104.0 0.8 copy.92
  (5 shorter events, 0.1 us)
Async XLA Ops:
  0.0 1.1 %copy-start.2 = (bf16[512,128]{1,0:T(8,128)(2,1)S(1)}, bf16[512,128]{1,0:T(8,128)(2,1)}, u32[]{:S(2)}) copy-start(bf16[512,128]{1,0:T(8,128)(2,1)} %param.7) | copy-start | bytes 393220
  0.0 27.0 %copy-start.1 = (f32[2,2,512,128]{3,2,1,0:T(8,128)S(1)}, f32[2,2,512,128]{3,2,1,0:T(8,128)}, u32[]{:S(2)}) copy-start(f32[2,2,512,128]{3,2,1,0:T(8,128)} %param.12) | copy-start | bytes 3145732
  12.1 26.1 %all-to-all-start = ((bf16[64,2,512]{2,1,0:T(2,128)(2,1)}), bf16[64,2,512]{2,1,0:T(2,128)(2,1)S(1)}, u32[]{:S(2)}, u32[]{:S(2)}) async-start(bf16[64,2,512]{2,1,0:T(2,128)(2,1)} %all_to_all.37), calls=%async_computation | async-start | bytes 262144 | tf_op jit(solution)/shard_map/all_to_all | solution.py:49
  28.4 14.3 %copy-start.4 = (s32[512]{0:T(512)S(1)}, s32[512]{0:T(512)}, u32[]{:S(2)}) copy-start(s32[512]{0:T(512)} %constant.60.clone) | copy-start | bytes 6148
  38.2 32.6 %all-to-all-start.1 = ((f32[128,2,2,4,128]{4,3,2,1,0:T(4,128)}), f32[128,2,2,4,128]{4,3,2,1,0:T(4,128)S(1)}, u32[]{:S(2)}, u32[]{:S(2)}) async-start(f32[128,2,2,4,128]{4,3,2,1,0:T(4,128)} %copy.81), calls=%async_computation.1 | async-start | bytes 2097152 | tf_op jit(solution)/shard_map/all_to_all | solution.py:43
  71.1 1.0 copy-start
  83.5 6.5 %copy-start.3 = (bf16[512,128]{1,0:T(8,128)(2,1)S(1)}, bf16[512,128]{1,0:T(8,128)(2,1)}, u32[]{:S(2)}) copy-start(bf16[512,128]{1,0:T(8,128)(2,1)} %param.9) | copy-start | bytes 393220
  83.5 19.7 %all-to-all-start.2 = ((f32[2,64,512]{2,0,1:T(2,128)}), f32[2,64,512]{2,0,1:T(2,128)S(1)}, u32[]{:S(2)}, u32[]{:S(2)}) async-start(f32[2,64,512]{2,0,1:T(2,128)} %copy.91), calls=%async_computation.2 | async-start | bytes 524288 | tf_op jit(solution)/shard_map/all_to_all | solution.py:77
  103.2 0.7 copy-start.5
  103.2 0.7 copy-start.6
